TPU v7x, 256 devices: a whole 4x4x8 slice. The times are simulated.
256 devices in a mesh: layer: 8 (over y_lo, x), feat: 32 (over z, y_hi, core).
Axes of the slice: x: 4, y: 4 (y_hi: 2, y_lo: 2; y = y_hi * 2 + y_lo), z: 8, core: 2. Of those that a mesh axis runs over, the one named last changes fastest.
Arguments:
- inputs: bfloat16 [8, 128, 2304], P('layer'), may hold values from -6 to 6
- targets: bfloat16 [8, 128, 2304], P('layer', None, 'feat'), may hold values from -6 to 6
- w_enc: bfloat16 [8, 2304, 2048], P('layer', None, 'feat'), may hold values from -0.125 to 0.125
- b_enc: float32 [8, 2048], P('layer', 'feat'), may hold values from -3 to 3
- w_dec: bfloat16 [8, 8, 2048, 2304], P('layer', None, 'feat'), may hold values from -0.046875 to 0.046875
Outputs:
- grad_enc: bfloat16 [8, 2304, 2048], P('layer', None, 'feat')
- grad_dec: bfloat16 [8, 8, 2048, 2304], P('layer', None, 'feat')
- grad_benc: float32 [8, 2048], P('layer', 'feat')
All inputs are finite; a program needn't handle non-finite values.
Results may differ from a plain program's by a relative error of at most 0.0085.
Values may be sent and summed in bfloat16 or wider, within the bound.
A program may use at most 64 MiB of HBM per device.

v0:
```python
import jax
import jax.numpy as jnp
from jax import lax
from jax.sharding import PartitionSpec as P


def shards(inputs, targets, w_enc, b_enc, w_dec):
    layer_count = w_dec.shape[1]
    feat_count = lax.axis_size("feat")
    tok_count = inputs.shape[1]
    model_width = inputs.shape[2]
    col_count = model_width // feat_count
    slab_width = w_dec.shape[2]
    grad_scale = tok_count ** (-0.5)
    own_layer = lax.axis_index("layer")
    pre_act = jnp.dot(inputs[0], w_enc[0], preferred_element_type=jnp.float32) + b_enc[0]
    active = jax.nn.relu(pre_act).astype(jnp.bfloat16)
    later_mask = jnp.arange(layer_count) >= own_layer
    later_float = later_mask.astype(jnp.float32)
    later_half = later_mask.astype(jnp.bfloat16)
    weights = w_dec[0]
    blocks = weights.reshape(layer_count, slab_width, feat_count, col_count)
    partials = jnp.einsum("tf,mfnc->mntc", active, blocks, preferred_element_type=jnp.float32)
    partials = partials * later_float[:, None, None, None]
    partials = partials.reshape(layer_count * feat_count, tok_count, col_count)
    rebuilt = lax.psum_scatter(partials, ("layer", "feat"), scatter_dimension=0, tiled=True)[0]
    errors = (rebuilt - targets[0].astype(jnp.float32)).astype(jnp.bfloat16)
    err_block = errors[None, None]
    everything = lax.all_gather(err_block, ("layer", "feat"), axis=0, tiled=True)
    everything = everything.reshape(layer_count, feat_count, tok_count, col_count)
    masked = everything * later_half[:, None, None, None]
    act_grad = grad_scale * jnp.einsum(
        "mntc,mfnc->tf", masked, blocks, preferred_element_type=jnp.float32
    )
    dec_grad = (
        jnp.einsum("tf,mntc->mfnc", active, masked, preferred_element_type=jnp.float32) * grad_scale
    )
    grad_dec = dec_grad.astype(jnp.bfloat16).reshape(layer_count, slab_width, model_width)
    pre_grad = jnp.where(pre_act > 0, act_grad, 0.0).astype(jnp.bfloat16)
    grad_enc = jnp.einsum(
        "td,tf->df", inputs[0], pre_grad, preferred_element_type=jnp.float32
    ).astype(jnp.bfloat16)
    grad_benc = jnp.sum(pre_grad.astype(jnp.float32), axis=0)
    return (grad_enc[None], grad_dec[None], grad_benc[None])


def solution(mesh):
    in_specs = (
        P("layer", None, None),
        P("layer", None, "feat"),
        P("layer", None, "feat"),
        P("layer", "feat"),
        P("layer", None, "feat", None),
    )
    out_specs = (P("layer", None, "feat"), P("layer", None, "feat", None), P("layer", "feat"))
    return jax.shard_map(shards, mesh=mesh, in_specs=in_specs, out_specs=out_specs, check_vma=False)
```

profile of v0, /device:TPU:32, one launch (start us, length us, event | category | flops | bytes accessed | tf_op | source)
XLA Modules:
  0.0 1771.0 jit_solution(4785494572840686136)
XLA Ops:
  7.2 0.0 copy-start
  7.2 0.0 copy-start.4
  7.2 0.0 copy-start.2
  7.2 0.0 reduce-scatter.5.cloned.1.call-start
  7.3 11.4 reshape_squeeze.3
  18.6 0.0 copy-done
  18.6 0.0 copy-done.4
  18.6 0.0 copy-done.2
  18.6 0.3 convolution_add_fusion
  19.0 8.7 broadcast_multiply_fusion
  27.6 0.0 copy-start.3
  27.7 0.0 reduce-scatter.5.cloned.1.call-update
  27.7 0.2 all-gather.3.cloned.1.call-start
  27.9 1287.9 %reduce-scatter.5.cloned.1.call-done = f32[1,128,72]{1,2,0:T(8,128)} async-done(((f32[256,128,72]{1,2,0:T(8,128)}), f32[1,128,72]{1,2,0:T(8,128)}) %reduce-scatter.5.cloned.1.call-update) | async-done | bytes 36880
  1315.8 0.0 copy-done.3
  1315.8 1.4 subtract_convert_fusion
  1317.2 0.0 all-gather.3.cloned.1.call-update
  1317.3 421.7 %all-gather.3.cloned.1.call-done = bf16[256,128,72]{1,2,0:T(8,128)(2,1)} async-done(((bf16[1,128,72]{1,2,0:T(8,128)(2,1)}), bf16[256,128,72]{1,2,0:T(8,128)(2,1)}) %all-gather.3.cloned.1.call-update) | async-done | bytes 4718608 | tf_op jit(solution)/shard_map/all_gather | solution.py:29
  1738.9 0.0 copy-start.1
  1738.9 7.0 convert_reduce_fusion
  1746.0 0.0 copy-done.1
  1746.0 4.3 fusion
  1750.3 4.8 copy.15
  1755.1 8.1 broadcast_in_dim_reshape.3
  1763.2 0.9 fusion.10
  (2 shorter events, 0.0 us)
Async XLA Ops:
  7.2 11.5 copy-start
  7.2 11.4 copy-start.4
  7.2 11.4 copy-start.2
  7.2 1308.6 %reduce-scatter.5.cloned.1.call-start = ((), (), s32[]{:S(2)}) async-start(), calls=%async_computation.2 | async-start | bytes 9474048
  27.6 1288.2 %copy-start.3 = (bf16[1,128,72]{1,2,0:T(8,128)(2,1)S(1)}, bf16[1,128,72]{1,2,0:T(8,128)(2,1)}, u32[]{:S(2)}) copy-start(bf16[1,128,72]{1,2,0:T(8,128)(2,1)} %param.6) | copy-start | bytes 55300
  27.7 1711.3 %all-gather.3.cloned.1.call-start = ((), (), s32[]{:S(2)}) async-start(), calls=%async_computation.1 | async-start | bytes 4737024 | tf_op jit(solution)/shard_map/all_gather | solution.py:29
  1738.9 7.0 copy-start.1
Sparse Core Ops, SparseCore 0:
  27.8 1287.9 reduce-scatter.4
  1318.3 420.5 all-gather.2
where the time goes:
time: 1770 us
  waiting for transfers between devices  1710 us (97%)
  local copies, waits for them, and re-layouts  24.3 us (1%)
  matrix products  21.3 us (1%)
    unnamed x3, waiting for transfers between devices  1290 us
    all_gather x1, waiting for transfers between devices, shards(): lax.all_gather(err_block, ('layer', 'feat'), axis=0, tiled=True)  422 us
  transfers between devices with their start and end apart: 2, of which 2 were waited for; matrix products, arithmetic and copies ran while one was open for 0% of the time, Pallas kernels for 0%

commit v1 on v0

--- a/solution.py
+++ b/solution.py
@@ -26,7 +26,12 @@
     rebuilt = lax.psum_scatter(partials, ("layer", "feat"), scatter_dimension=0, tiled=True)[0]
     errors = (rebuilt - targets[0].astype(jnp.float32)).astype(jnp.bfloat16)
     err_block = errors[None, None]
-    everything = lax.all_gather(err_block, ("layer", "feat"), axis=0, tiled=True)
+    everything = jnp.concatenate(
+        lax.all_to_all(
+            jnp.stack([err_block] * lax.axis_size(("layer", "feat"))), ("layer", "feat"), 0, 0
+        ),
+        axis=0,
+    )
     everything = everything.reshape(layer_count, feat_count, tok_count, col_count)
     masked = everything * later_half[:, None, None, None]
     act_grad = grad_scale * jnp.einsum(

time: 1770 us -> 1490 us (0.84)
  waiting for transfers between devices: 1710 us -> 1400 us
  starting transfers between devices: 0.26 us -> 19.3 us
    all_gather x1 -> x0, waiting for transfers between devices: 422 us -> none  [shards(): lax.all_gather(err_block, ('layer', 'feat'), axis=0, tiled=True)]
    all_to_all x0 -> x1, waiting for transfers between devices: none -> 107 us  [shards(): lax.all_to_all(jnp.stack([err_block] * lax.axis_size(('layer', 'feat'))),...]
    all_to_all x0 -> x1, starting transfers between devices: none -> 19.2 us  [shards(): lax.all_to_all(jnp.stack([err_block] * lax.axis_size(('layer', 'feat'))),...]
    unnamed x3 -> x2, waiting for transfers between devices: 1290 us -> 1290 us
where the time goes in v1:
time: 1490 us; the launch traced here: 1480 us
  waiting for transfers between devices  1400 us (94%)
  local copies, waits for them, and re-layouts  27 us (2%)
  matrix products  23.5 us (2%)
  starting transfers between devices  19.3 us (1%)
    unnamed x2, waiting for transfers between devices  1290 us
    all_to_all x1, waiting for transfers between devices, shards(): lax.all_to_all(jnp.stack([err_block] * lax.axis_size(('layer', 'feat'))),...  107 us
  transfers between devices with their start and end apart: 2, of which 2 were waited for; matrix products, arithmetic and copies ran while one was open for 0% of the time, Pallas kernels for 0%

profile of v1, /device:TPU:32, one launch (start us, length us, event | category | flops | bytes accessed | tf_op | source)
XLA Modules:
  0.0 1483.4 jit_solution(3741980360788733408)
XLA Ops:
  7.2 0.0 copy-start
  7.2 0.0 copy-start.3
  7.2 0.0 copy-start.1
  7.2 0.0 reduce-scatter.5.cloned.1.call-start
  7.3 11.3 reshape_squeeze.3
  18.6 0.0 copy-done
  18.6 0.0 copy-done.3
  18.6 0.0 copy-done.1
  18.6 0.3 convolution_add_fusion
  19.0 8.7 broadcast_multiply_fusion
  27.6 0.0 copy-start.2
  27.6 0.0 reduce-scatter.5.cloned.1.call-update
  27.7 1291.6 %reduce-scatter.5.cloned.1.call-done = f32[1,128,72]{1,2,0:T(8,128)} async-done(((f32[256,128,72]{1,2,0:T(8,128)}), f32[1,128,72]{1,2,0:T(8,128)}) %reduce-scatter.5.cloned.1.call-update) | async-done | bytes 36880
  1319.3 0.0 copy-done.2
  1319.3 0.8 fusion.38
  1320.1 2.8 stack.3
  1322.8 19.2 %all-to-all-start = ((bf16[256,1,1,128,72]{3,4,2,1,0:T(8,128)(2,1)}), bf16[256,1,1,128,72]{3,4,2,1,0:T(8,128)(2,1)}, u32[]{:S(2)}, u32[]{:S(2)}) async-start(bf16[256,1,1,128,72]{3,4,2,1,0:T(8,128)(2,1)} %stack.3), calls=%async_computation | async-start | bytes 9437184 | tf_op jit(solution)/shard_map/all_to_all | solution.py:30
  1342.1 107.0 %all-to-all-done = bf16[256,1,1,128,72]{3,4,2,1,0:T(8,128)(2,1)} async-done(((bf16[256,1,1,128,72]{3,4,2,1,0:T(8,128)(2,1)}), bf16[256,1,1,128,72]{3,4,2,1,0:T(8,128)(2,1)}, u32[]{:S(2)}, u32[]{:S(2)}) %all-to-all-start) | async-done | bytes 4718624 | tf_op jit(solution)/shard_map/all_to_all | solution.py:30
  1449.1 6.9 convert_reduce_fusion
  1456.0 6.7 fusion
  1462.7 4.8 copy.15
  1467.5 8.1 broadcast_in_dim_reshape.3
  1475.6 0.9 fusion.10
  (2 shorter events, 0.0 us)
Async XLA Ops:
  7.2 11.4 copy-start
  7.2 11.4 copy-start.3
  7.2 11.4 copy-start.1
  7.2 1312.1 %reduce-scatter.5.cloned.1.call-start = ((), (), s32[]{:S(2)}) async-start(), calls=%async_computation.2 | async-start | bytes 9474048
  27.6 1291.6 %copy-start.2 = (bf16[1,128,72]{1,2,0:T(8,128)(2,1)S(1)}, bf16[1,128,72]{1,2,0:T(8,128)(2,1)}, u32[]{:S(2)}) copy-start(bf16[1,128,72]{1,2,0:T(8,128)(2,1)} %param.6) | copy-start | bytes 55300
  1322.8 126.3 %all-to-all-start = ((bf16[256,1,1,128,72]{3,4,2,1,0:T(8,128)(2,1)}), bf16[256,1,1,128,72]{3,4,2,1,0:T(8,128)(2,1)}, u32[]{:S(2)}, u32[]{:S(2)}) async-start(bf16[256,1,1,128,72]{3,4,2,1,0:T(8,128)(2,1)} %stack.3), calls=%async_computation | async-start | bytes 9437184 | tf_op jit(solution)/shard_map/all_to_all | solution.py:30
Sparse Core Ops, SparseCore 0:
  27.8 1291.4 reduce-scatter.4
